TPU v7x, 32 devices: a whole 2x2x4 slice. The times are simulated.
32 devices in a mesh: pipe: 4 (over x, core), tensor: 8 (over z, y).
Axes of the slice: x: 2, y: 2, z: 4, core: 2. Of those that a mesh axis runs over, the one named last changes fastest.
Arguments:
- hidden: bfloat16 [384, 8192], P('pipe', 'tensor'), may hold values from -64 to 64
- weight: bfloat16 [8192, 16384], P(None, ('pipe', 'tensor')), may hold values from -0.23201941 to 0.23201941
- targets: int32 [384], replicated, may hold values from 0 to 16383
- token_weight: float32 [384], replicated, may hold values from 0.1 to 1
Outputs:
- token_loss: float32 [384], P('pipe')
- hidden_grad: float32 [384, 8192], P('pipe', 'tensor')
All inputs are finite; a program needn't handle non-finite values.
Results may differ from a plain program's by a relative error of at most 0.0029.
Values may be sent and summed in bfloat16 or wider, within the bound.
A program may use at most 128 MiB of HBM per device.

v0:
```python
import jax
import jax.numpy as jnp
from jax import lax
from jax.sharding import PartitionSpec as P

loss_scale = 32.0


def local(hidden, weight, targets, token_weight):
    rows_local = hidden.shape[0]
    width_local = weight.shape[1]
    full_rows = lax.all_gather(hidden, "tensor", axis=1, tiled=True)
    logits = jnp.dot(
        lax.all_gather(full_rows, "pipe", axis=0, tiled=True),
        weight,
        preferred_element_type=jnp.float32,
    )
    device_block = lax.axis_index("pipe") * lax.axis_size("tensor") + lax.axis_index("tensor")
    columns = device_block * width_local + jnp.arange(width_local, dtype=jnp.int32)
    target_hit = targets[:, None] == columns[None, :]
    chosen = jnp.sum(jnp.where(target_hit, logits, jnp.float32(0.0)), axis=1)
    local_peak = jnp.max(logits, axis=1)
    global_peak = lax.pmax(local_peak, ("pipe", "tensor"))
    local_total = jnp.sum(jnp.exp(logits - global_peak[:, None]), axis=1)
    global_total, target_logit = lax.psum((local_total, chosen), ("pipe", "tensor"))
    log_total = global_peak + jnp.log(global_total)
    loss_rows = log_total - target_logit
    token_loss = lax.dynamic_slice_in_dim(
        loss_rows, lax.axis_index("pipe") * rows_local, rows_local, 0
    )
    softmax = jnp.exp(logits - log_total[:, None])
    dlogits = (
        loss_scale * token_weight[:, None] * (softmax - target_hit.astype(jnp.float32))
    ).astype(jnp.bfloat16)
    section_part = lax.psum_scatter(
        lax.dot_general(
            dlogits, weight, (((1,), (1,)), ((), ())), preferred_element_type=jnp.float32
        ),
        "pipe",
        scatter_dimension=0,
        tiled=True,
    )
    hidden_grad = lax.psum_scatter(section_part, "tensor", scatter_dimension=1, tiled=True)
    return (token_loss, hidden_grad)


def solution(mesh):
    in_specs = (P("pipe", "tensor"), P(None, ("pipe", "tensor")), P(), P())
    out_specs = (P("pipe"), P("pipe", "tensor"))
    return jax.shard_map(local, mesh=mesh, in_specs=in_specs, out_specs=out_specs, check_vma=False)
```

profile of v0, /device:TPU:0, one launch (start us, length us, event | category | flops | bytes accessed | tf_op | source)
XLA Modules:
  0.0 389.2 jit_solution(3919256009394892303)
XLA Ops:
  7.2 0.0 all-gather.3.cloned.1.call-start
  7.2 0.7 all-gather.3.cloned.1.call-update
  7.9 0.0 all-gather.5.cloned.1.call-start
  7.9 49.2 %all-gather.3.cloned.1.call-done = bf16[96,8192]{1,0:T(8,128)(2,1)} async-done(((bf16[96,1024]{1,0:T(8,128)(2,1)}), bf16[96,8192]{1,0:T(8,128)(2,1)}) %all-gather.3.cloned.1.call-update) | async-done | bytes 1572880 | tf_op jit(solution)/shard_map/all_gather | solution.py:12
  57.1 0.0 all-gather.5.cloned.1.call-update
  57.1 0.0 reduce-scatter.3.cloned.1.call-start
  57.2 0.7 broadcast_multiply_fusion
  57.9 0.0 copy-start
  57.9 45.5 %all-gather.5.cloned.1.call-done = bf16[384,8192]{1,0:T(8,128)(2,1)} async-done(((bf16[96,8192]{1,0:T(8,128)(2,1)}), bf16[384,8192]{1,0:T(8,128)(2,1)}) %all-gather.5.cloned.1.call-update) | async-done | bytes 6291472 | tf_op jit(solution)/shard_map/all_gather | solution.py:14
  103.4 8.0 %fusion.11 = (f32[384]{0:T(512)S(1)}, f32[384,512]{1,0:T(8,128)S(1)}) fusion(bf16[384,8192]{1,0:T(8,128)(2,1)} %all-gather.5.cloned.1.call-done, bf16[8192,512]{1,0:T(8,128)(2,1)} %param.5), kind=kOutput, calls=%fused_computation.16 | convolution fusion | flops 3221421568 | bytes 15468032 | tf_op jit(solution)/shard_map/dot_general | solution.py:13
  111.4 39.3 %pmax.7 = f32[384]{0:T(512)S(1)} all-reduce(f32[384]{0:T(512)S(1)} %get-tuple-element.8), channel_id=1, replica_groups=mesh['pipe'=4,'tensor'=8] {'pipe','tensor'}, use_global_device_ids=true, to_apply=%region_1.2 | all-reduce | flops 384 | bytes 3072 | tf_op jit(solution)/shard_map/pmax | solution.py:23
  150.7 0.0 copy-done
  150.7 0.3 fusion
  151.1 41.0 %all-reduce = (f32[384]{0:T(512)S(1)}, f32[384]{0:T(512)S(1)}) all-reduce(f32[384]{0:T(512)S(1)} %get-tuple-element.3, f32[384]{0:T(512)S(1)} %get-tuple-element.2), channel_id=1, replica_groups=mesh['pipe'=4,'tensor'=8] {'pipe','tensor'}, use_global_device_ids=true, to_apply=%region_3.4 | all-reduce | flops 768 | bytes 6144 | tf_op jit(solution)/shard_map/psum | solution.py:25
  192.1 12.0 %fusion.4 = f32[384,8192]{1,0:T(8,128)} fusion(bf16[8192,512]{1,0:T(8,128)(2,1)} %param.5, f32[384,512]{1,0:T(8,128)S(1)} %get-tuple-element.9, f32[384]{0:T(512)S(1)} %get-tuple-element.7, f32[384]{0:T(512)S(1)} %broadcast_multiply_fusion, s32[512]{0:T(512)S(1)} %iota_add_fusion, s32[384]{0:T(512)S(1)} %copy-done), kind=kOutput, calls=%fused_computation.7 | convolution fusion | flops 3222405120 | bytes 21764608 | tf_op jit(solution)/shard_map/dot_general | solution.py:36
  204.1 0.0 reduce-scatter.3.cloned.1.call-update
  204.1 0.0 reduce-scatter.5.cloned.1.call-start
  204.1 99.5 %reduce-scatter.3.cloned.1.call-done = f32[96,8192]{1,0:T(8,128)} async-done(((f32[384,8192]{1,0:T(8,128)}), f32[96,8192]{1,0:T(8,128)}) %reduce-scatter.3.cloned.1.call-update) | async-done | bytes 3145744 | tf_op jit(solution)/shard_map/reduce_scatter | solution.py:35
  303.6 0.0 reduce-scatter.5.cloned.1.call-update
  303.6 0.6 dynamic_slice.3
  304.2 78.4 %reduce-scatter.5.cloned.1.call-done = f32[96,1024]{1,0:T(8,128)} async-done(((f32[96,8192]{1,0:T(8,128)}), f32[96,1024]{1,0:T(8,128)}) %reduce-scatter.5.cloned.1.call-update) | async-done | bytes 393232 | tf_op jit(solution)/shard_map/reduce_scatter | solution.py:43
  (2 shorter events, 0.0 us)
Async XLA Ops:
  7.2 49.9 %all-gather.3.cloned.1.call-start = ((), (), s32[]{:S(2)}) async-start(), calls=%async_computation.2 | async-start | bytes 1769472 | tf_op jit(solution)/shard_map/all_gather | solution.py:12
  7.9 95.5 %all-gather.5.cloned.1.call-start = ((), (), s32[]{:S(2)}) async-start(), calls=%async_computation.3 | async-start | bytes 7864320 | tf_op jit(solution)/shard_map/all_gather | solution.py:14
  57.1 246.5 %reduce-scatter.3.cloned.1.call-start = ((), (), s32[]{:S(2)}) async-start(), calls=%async_computation.4 | async-start | bytes 15728640 | tf_op jit(solution)/shard_map/reduce_scatter | solution.py:35
  57.9 92.9 %copy-start = (s32[384]{0:T(512)S(1)}, s32[384]{0:T(512)}, u32[]{:S(2)}) copy-start(s32[384]{0:T(512)} %param.6) | copy-start | bytes 4612
  204.1 178.6 %reduce-scatter.5.cloned.1.call-start = ((), (), s32[]{:S(2)}) async-start(), calls=%async_computation.5 | async-start | bytes 3538944 | tf_op jit(solution)/shard_map/reduce_scatter | solution.py:43
Sparse Core Ops, SparseCore 0:
  10.2 46.9 all-gather.2
  58.7 44.7 all-gather.4
  204.2 99.3 reduce-scatter.2
  307.7 74.9 reduce-scatter.4
where the time goes:
time: 390 us; the launch traced here: 389 us
  waiting for transfers between devices  273 us (70%)
  blocking collectives  80.3 us (21%)
  matrix products  20 us (5%)
  between operations  13.8 us (4%)
    reduce_scatter x1, waiting for transfers between devices, local(): lax.psum_scatter(lax.dot_general(dlogits, weight, (((1,), (1,)), ((), ())...  99.5 us
    reduce_scatter x1, waiting for transfers between devices, local(): lax.psum_scatter(section_part, 'tensor', scatter_dimension=1, tiled=True)  78.4 us
    all_gather x1, waiting for transfers between devices, local(): full_rows = lax.all_gather(hidden, 'tensor', axis=1, tiled=True)  49.2 us
    all_gather x1, waiting for transfers between devices, local(): lax.all_gather(full_rows, 'pipe', axis=0, tiled=True)  45.5 us
    psum x1, blocking collectives, local(): lax.psum((local_total, chosen), ('pipe', 'tensor'))  41 us
    pmax x1, blocking collectives, local(): global_peak = lax.pmax(local_peak, ('pipe', 'tensor'))  39.3 us
    dot_general x1, matrix products, local(): lax.dot_general(dlogits, weight, (((1,), (1,)), ((), ())), preferred_elem...  12 us
    dot_general x1, matrix products, local(): jnp.dot(lax.all_gather(full_rows, 'pipe', axis=0, tiled=True), weight, pr...  8 us
  transfers between devices with their start and end apart: 4, of which 4 were waited for; matrix products, arithmetic and copies ran while one was open for 0% of the time, Pallas kernels for 0%

commit v1 on v0

--- a/solution.py
+++ b/solution.py
@@ -9,7 +9,14 @@
 def local(hidden, weight, targets, token_weight):
     rows_local = hidden.shape[0]
     width_local = weight.shape[1]
-    full_rows = lax.all_gather(hidden, "tensor", axis=1, tiled=True)
+    ring = [hidden]
+    for hop in range(7):
+        ring.append(lax.ppermute(ring[-1], "tensor", [(dev, (dev + 1) % 8) for dev in range(8)]))
+    full_rows = jnp.roll(
+        jnp.concatenate(ring[::-1], axis=1),
+        (lax.axis_index("tensor") + 1) * ring[0].shape[1],
+        axis=1,
+    )
     logits = jnp.dot(
         lax.all_gather(full_rows, "pipe", axis=0, tiled=True),
         weight,

time: 390 us -> 403 us (1.033)
  waiting for transfers between devices: 273 us -> 282 us
    ppermute x0 -> x7, waiting for transfers between devices: none -> 59.6 us  [local(): lax.ppermute(ring[-1], 'tensor', [(dev, (dev + 1) % 8) for dev in range(8)])]
    all_gather x1 -> x0, waiting for transfers between devices: 49.2 us -> none  [local(): full_rows = lax.all_gather(hidden, 'tensor', axis=1, tiled=True)]
  transfers between devices with their start and end apart: 4 -> 10, of which waited for: 4 -> 10; matrix products, arithmetic and copies ran while one was open for 0% -> 0% of each run, Pallas kernels for 0% -> 0%
where the time goes in v1:
time: 403 us; the launch traced here: 402 us
  waiting for transfers between devices  282 us (70%)
  blocking collectives  80.3 us (20%)
  matrix products  20 us (5%)
  between operations  13.9 us (3%)
    reduce_scatter x1, waiting for transfers between devices, local(): lax.psum_scatter(lax.dot_general(dlogits, weight, (((1,), (1,)), ((), ())...  99.7 us
    reduce_scatter x1, waiting for transfers between devices, local(): lax.psum_scatter(section_part, 'tensor', scatter_dimension=1, tiled=True)  78.6 us
    ppermute x7, waiting for transfers between devices, local(): lax.ppermute(ring[-1], 'tensor', [(dev, (dev + 1) % 8) for dev in range(8)])  59.6 us
    all_gather x1, waiting for transfers between devices, local(): lax.all_gather(full_rows, 'pipe', axis=0, tiled=True)  43.7 us
    psum x1, blocking collectives, local(): lax.psum((local_total, chosen), ('pipe', 'tensor'))  41 us
    pmax x1, blocking collectives, local(): global_peak = lax.pmax(local_peak, ('pipe', 'tensor'))  39.3 us
    dot_general x1, matrix products, local(): lax.dot_general(dlogits, weight, (((1,), (1,)), ((), ())), preferred_elem...  12 us
  transfers between devices with their start and end apart: 10, of which 10 were waited for; matrix products, arithmetic and copies ran while one was open for 0% of the time, Pallas kernels for 0%

profile of v1, /device:TPU:0, one launch (start us, length us, event | category | flops | bytes accessed | tf_op | source)
XLA Modules:
  0.0 402.4 jit_solution(2642962131138157066)
XLA Ops:
  7.2 0.0 copy-start
  7.2 0.0 all-gather.2.cloned.1.call-start
  7.2 3.0 collective-permute-start
  10.3 8.2 %collective-permute-done = bf16[96,1024]{1,0:T(8,128)(2,1)S(1)} collective-permute-done((bf16[96,1024]{1,0:T(8,128)(2,1)}, bf16[96,1024]{1,0:T(8,128)(2,1)S(1)}, u32[]{:S(2)}, u32[]{:S(2)}) %collective-permute-start) | collective-permute-done | bytes 196640 | tf_op jit(solution)/shard_map/ppermute | solution.py:14
  18.4 0.0 collective-permute-start.1
  18.4 8.8 %collective-permute-done.1 = bf16[96,1024]{1,0:T(8,128)(2,1)S(1)} collective-permute-done((bf16[96,1024]{1,0:T(8,128)(2,1)S(1)}, bf16[96,1024]{1,0:T(8,128)(2,1)S(1)}, u32[]{:S(2)}, u32[]{:S(2)}) %collective-permute-start.1) | collective-permute-done | bytes 196640 | tf_op jit(solution)/shard_map/ppermute | solution.py:14
  27.2 0.0 collective-permute-start.2
  27.2 8.4 %collective-permute-done.2 = bf16[96,1024]{1,0:T(8,128)(2,1)S(1)} collective-permute-done((bf16[96,1024]{1,0:T(8,128)(2,1)S(1)}, bf16[96,1024]{1,0:T(8,128)(2,1)S(1)}, u32[]{:S(2)}, u32[]{:S(2)}) %collective-permute-start.2) | collective-permute-done | bytes 196640 | tf_op jit(solution)/shard_map/ppermute | solution.py:14
  35.6 0.0 collective-permute-start.3
  35.6 8.4 %collective-permute-done.3 = bf16[96,1024]{1,0:T(8,128)(2,1)S(1)} collective-permute-done((bf16[96,1024]{1,0:T(8,128)(2,1)S(1)}, bf16[96,1024]{1,0:T(8,128)(2,1)S(1)}, u32[]{:S(2)}, u32[]{:S(2)}) %collective-permute-start.3) | collective-permute-done | bytes 196640 | tf_op jit(solution)/shard_map/ppermute | solution.py:14
  43.9 0.0 collective-permute-start.4
  43.9 8.4 %collective-permute-done.4 = bf16[96,1024]{1,0:T(8,128)(2,1)S(1)} collective-permute-done((bf16[96,1024]{1,0:T(8,128)(2,1)S(1)}, bf16[96,1024]{1,0:T(8,128)(2,1)S(1)}, u32[]{:S(2)}, u32[]{:S(2)}) %collective-permute-start.4) | collective-permute-done | bytes 196640 | tf_op jit(solution)/shard_map/ppermute | solution.py:14
  52.3 0.0 collective-permute-start.5
  52.3 9.3 %collective-permute-done.5 = bf16[96,1024]{1,0:T(8,128)(2,1)S(1)} collective-permute-done((bf16[96,1024]{1,0:T(8,128)(2,1)S(1)}, bf16[96,1024]{1,0:T(8,128)(2,1)S(1)}, u32[]{:S(2)}, u32[]{:S(2)}) %collective-permute-start.5) | collective-permute-done | bytes 196640 | tf_op jit(solution)/shard_map/ppermute | solution.py:14
  61.6 0.0 collective-permute-start.6
  61.6 8.4 %collective-permute-done.6 = bf16[96,1024]{1,0:T(8,128)(2,1)S(1)} collective-permute-done((bf16[96,1024]{1,0:T(8,128)(2,1)S(1)}, bf16[96,1024]{1,0:T(8,128)(2,1)S(1)}, u32[]{:S(2)}, u32[]{:S(2)}) %collective-permute-start.6) | collective-permute-done | bytes 196640 | tf_op jit(solution)/shard_map/ppermute | solution.py:14
  70.1 0.9 constant_dynamic-update-slice_fusion.8
  71.1 0.0 copy-start.2
  71.2 0.0 copy-done
  71.2 1.3 constant_dynamic-slice_fusion
  72.5 0.0 all-gather.2.cloned.1.call-update
  72.5 0.0 reduce-scatter.3.cloned.1.call-start
  72.6 0.0 copy-done.2
  72.6 0.0 copy-start.1
  72.6 43.7 %all-gather.2.cloned.1.call-done = bf16[384,8192]{1,0:T(8,128)(2,1)} async-done(((bf16[96,8192]{1,0:T(8,128)(2,1)}), bf16[384,8192]{1,0:T(8,128)(2,1)}) %all-gather.2.cloned.1.call-update) | async-done | bytes 6291472 | tf_op jit(solution)/shard_map/all_gather | solution.py:21
  116.3 8.0 %fusion.11 = (f32[384]{0:T(512)S(1)}, f32[384,512]{1,0:T(8,128)S(1)}) fusion(bf16[384,8192]{1,0:T(8,128)(2,1)} %all-gather.2.cloned.1.call-done, bf16[8192,512]{1,0:T(8,128)(2,1)} %param.5), kind=kOutput, calls=%fused_computation.33 | convolution fusion | flops 3221421568 | bytes 15468032 | tf_op jit(solution)/shard_map/dot_general | solution.py:20
  124.3 39.3 %pmax.7 = f32[384]{0:T(512)S(1)} all-reduce(f32[384]{0:T(512)S(1)} %get-tuple-element.8), channel_id=1, replica_groups=mesh['pipe'=4,'tensor'=8] {'pipe','tensor'}, use_global_device_ids=true, to_apply=%region_1.2 | all-reduce | flops 384 | bytes 3072 | tf_op jit(solution)/shard_map/pmax | solution.py:30
  163.6 0.0 copy-done.1
  163.6 0.3 fusion
  164.0 41.0 %all-reduce = (f32[384]{0:T(512)S(1)}, f32[384]{0:T(512)S(1)}) all-reduce(f32[384]{0:T(512)S(1)} %get-tuple-element.3, f32[384]{0:T(512)S(1)} %get-tuple-element.2), channel_id=1, replica_groups=mesh['pipe'=4,'tensor'=8] {'pipe','tensor'}, use_global_device_ids=true, to_apply=%region_3.4 | all-reduce | flops 768 | bytes 6144 | tf_op jit(solution)/shard_map/psum | solution.py:32
  204.9 12.0 %fusion.4 = f32[384,8192]{1,0:T(8,128)} fusion(bf16[8192,512]{1,0:T(8,128)(2,1)} %param.5, f32[384,512]{1,0:T(8,128)S(1)} %get-tuple-element.9, f32[384]{0:T(512)S(1)} %get-tuple-element.7, f32[384]{0:T(512)S(1)} %broadcast_multiply_fusion, s32[512]{0:T(512)S(1)} %iota_add_fusion, s32[384]{0:T(512)S(1)} %copy-done.1), kind=kOutput, calls=%fused_computation.7 | convolution fusion | flops 3222405120 | bytes 21764608 | tf_op jit(solution)/shard_map/dot_general | solution.py:43
  216.9 0.0 reduce-scatter.3.cloned.1.call-update
  216.9 0.0 reduce-scatter.5.cloned.1.call-start
  217.0 99.7 %reduce-scatter.3.cloned.1.call-done = f32[96,8192]{1,0:T(8,128)} async-done(((f32[384,8192]{1,0:T(8,128)}), f32[96,8192]{1,0:T(8,128)}) %reduce-scatter.3.cloned.1.call-update) | async-done | bytes 3145744 | tf_op jit(solution)/shard_map/reduce_scatter | solution.py:42
  316.7 0.0 reduce-scatter.5.cloned.1.call-update
  316.7 0.6 dynamic_slice.8
  317.3 78.6 %reduce-scatter.5.cloned.1.call-done = f32[96,1024]{1,0:T(8,128)} async-done(((f32[96,8192]{1,0:T(8,128)}), f32[96,1024]{1,0:T(8,128)}) %reduce-scatter.5.cloned.1.call-update) | async-done | bytes 393232 | tf_op jit(solution)/shard_map/reduce_scatter | solution.py:50
  (18 shorter events, 0.2 us)
Async XLA Ops:
  7.2 64.0 %copy-start = (bf16[96,1024]{1,0:T(8,128)(2,1)S(1)}, bf16[96,1024]{1,0:T(8,128)(2,1)}, u32[]{:S(2)}) copy-start(bf16[96,1024]{1,0:T(8,128)(2,1)} %param.4) | copy-start | bytes 589828
  7.2 109.1 %all-gather.2.cloned.1.call-start = ((), (), s32[]{:S(2)}) async-start(), calls=%async_computation.2 | async-start | bytes 7864320 | tf_op jit(solution)/shard_map/all_gather | solution.py:21
  7.2 11.2 %collective-permute-start = (bf16[96,1024]{1,0:T(8,128)(2,1)}, bf16[96,1024]{1,0:T(8,128)(2,1)S(1)}, u32[]{:S(2)}, u32[]{:S(2)}) collective-permute-start(bf16[96,1024]{1,0:T(8,128)(2,1)} %param.4), channel_id=1, source_target_pairs={{0,1},{1,2},{2,3},{3,4},{4,5},{5,6},{6,7},{7,0},{8,9},{9,10},{10,1... | collective-permute-start | bytes 589832 | tf_op jit(solution)/shard_map/ppermute | solution.py:14
  18.4 8.8 %collective-permute-start.1 = (bf16[96,1024]{1,0:T(8,128)(2,1)S(1)}, bf16[96,1024]{1,0:T(8,128)(2,1)S(1)}, u32[]{:S(2)}, u32[]{:S(2)}) collective-permute-start(bf16[96,1024]{1,0:T(8,128)(2,1)S(1)} %collective-permute-done), channel_id=1, source_target_pairs={{0,1},{1,2},{2,3},{3,4},{4,5},{5,6},{6,7},{7,0},{8,9},{9,10},{10,1... | collective-permute-start | bytes 589832 | tf_op jit(solution)/shard_map/ppermute | solution.py:14
  27.2 8.4 %collective-permute-start.2 = (bf16[96,1024]{1,0:T(8,128)(2,1)S(1)}, bf16[96,1024]{1,0:T(8,128)(2,1)S(1)}, u32[]{:S(2)}, u32[]{:S(2)}) collective-permute-start(bf16[96,1024]{1,0:T(8,128)(2,1)S(1)} %collective-permute-done.1), channel_id=1, source_target_pairs={{0,1},{1,2},{2,3},{3,4},{4,5},{5,6},{6,7},{7,0},{8,9},{9,10},{10,1... | collective-permute-start | bytes 589832 | tf_op jit(solution)/shard_map/ppermute | solution.py:14
  35.6 8.4 %collective-permute-start.3 = (bf16[96,1024]{1,0:T(8,128)(2,1)S(1)}, bf16[96,1024]{1,0:T(8,128)(2,1)S(1)}, u32[]{:S(2)}, u32[]{:S(2)}) collective-permute-start(bf16[96,1024]{1,0:T(8,128)(2,1)S(1)} %collective-permute-done.2), channel_id=1, source_target_pairs={{0,1},{1,2},{2,3},{3,4},{4,5},{5,6},{6,7},{7,0},{8,9},{9,10},{10,1... | collective-permute-start | bytes 589832 | tf_op jit(solution)/shard_map/ppermute | solution.py:14
  43.9 8.4 %collective-permute-start.4 = (bf16[96,1024]{1,0:T(8,128)(2,1)S(1)}, bf16[96,1024]{1,0:T(8,128)(2,1)S(1)}, u32[]{:S(2)}, u32[]{:S(2)}) collective-permute-start(bf16[96,1024]{1,0:T(8,128)(2,1)S(1)} %collective-permute-done.3), channel_id=1, source_target_pairs={{0,1},{1,2},{2,3},{3,4},{4,5},{5,6},{6,7},{7,0},{8,9},{9,10},{10,1... | collective-permute-start | bytes 589832 | tf_op jit(solution)/shard_map/ppermute | solution.py:14
  52.3 9.3 %collective-permute-start.5 = (bf16[96,1024]{1,0:T(8,128)(2,1)S(1)}, bf16[96,1024]{1,0:T(8,128)(2,1)S(1)}, u32[]{:S(2)}, u32[]{:S(2)}) collective-permute-start(bf16[96,1024]{1,0:T(8,128)(2,1)S(1)} %collective-permute-done.4), channel_id=1, source_target_pairs={{0,1},{1,2},{2,3},{3,4},{4,5},{5,6},{6,7},{7,0},{8,9},{9,10},{10,1... | collective-permute-start | bytes 589832 | tf_op jit(solution)/shard_map/ppermute | solution.py:14
  61.6 8.4 %collective-permute-start.6 = (bf16[96,1024]{1,0:T(8,128)(2,1)S(1)}, bf16[96,1024]{1,0:T(8,128)(2,1)S(1)}, u32[]{:S(2)}, u32[]{:S(2)}) collective-permute-start(bf16[96,1024]{1,0:T(8,128)(2,1)S(1)} %collective-permute-done.5), channel_id=1, source_target_pairs={{0,1},{1,2},{2,3},{3,4},{4,5},{5,6},{6,7},{7,0},{8,9},{9,10},{10,1... | collective-permute-start | bytes 589832 | tf_op jit(solution)/shard_map/ppermute | solution.py:14
  71.1 1.5 copy-start.2
  72.5 244.2 %reduce-scatter.3.cloned.1.call-start = ((), (), s32[]{:S(2)}) async-start(), calls=%async_computation.3 | async-start | bytes 15728640 | tf_op jit(solution)/shard_map/reduce_scatter | solution.py:42
  72.6 91.0 %copy-start.1 = (s32[384]{0:T(512)S(1)}, s32[384]{0:T(512)}, u32[]{:S(2)}) copy-start(s32[384]{0:T(512)} %param.6) | copy-start | bytes 4612
  216.9 179.0 %reduce-scatter.5.cloned.1.call-start = ((), (), s32[]{:S(2)}) async-start(), calls=%async_computation.4 | async-start | bytes 3538944 | tf_op jit(solution)/shard_map/reduce_scatter | solution.py:50
Sparse Core Ops, SparseCore 0:
  72.6 43.5 all-gather.1
  217.1 99.6 reduce-scatter.2
  320.9 74.9 reduce-scatter.4
